TPU v7x, 32 devices: a whole 2x2x4 slice. The times are simulated.
32 devices in a mesh: dp: 2 (over x), tm: 2 (over y), space: 8 (over z, core).
Axes of the slice: x: 2, y: 2, z: 4, core: 2. Of those that a mesh axis runs over, the one named last changes fastest.
Arguments:
- latents: bfloat16 [32, 4, 128, 512], P(('dp', 'tm', 'space')), parts along dimension 0, may hold values from -36 to 36, as said below
- norm_gain: float32 [512], replicated, may hold values from 0.1 to 1.9
- conv_weight: bfloat16 [3, 3, 3, 512, 256], replicated, may hold values from -0.0546875 to 0.0546875
- skip_weight: bfloat16 [512, 256], replicated, may hold values from -0.25 to 0.25
- cotangent: bfloat16 [32, 8, 4, 16, 256], P(('dp', 'tm'), 'space'), parts along dimension 0, may hold values from -6 to 6
Outputs:
- output: bfloat16 [32, 8, 4, 16, 256], P(('dp', 'tm'), 'space'), parts along dimension 0
- grad_input: bfloat16 [32, 8, 4, 16, 512], P(('dp', 'tm'), 'space'), parts along dimension 0
There are 2 independent parts, one for each index of `dp`. A program takes and returns all parts, laid end to end along the dimension named above; an argument that names none is the same for every part. Nothing has to cross between parts.
Inputs may be any that keep to these rules, and one draw needn't show every extreme that they name: `latents`: each cell and each channel has its own scale.
All inputs are finite; a program needn't handle non-finite values.
Results may differ from a plain program's by a relative error of at most 0.002.
Values may be sent and summed in bfloat16 or wider, within the bound.
No kernel may reach another device: no remote copies, remote signals or barrier semaphores. Data moves between devices by JAX's collectives and lax.ppermute only.
A program may use at most 192 MiB of HBM per device.

v0:
```python
import jax
import jax.numpy as jnp
from jax import lax
from jax.sharding import PartitionSpec as P

epsilon = 1e-06


def extended_2(block, sides, width):
    for axis, dim in sides:
        count = lax.axis_size(axis)
        forward = [(i, i + 1) for i in range(count - 1)]
        backward = [(target, source) for source, target in forward]
        low = lax.ppermute(
            lax.slice_in_dim(block, block.shape[dim] - width, None, axis=dim), axis, forward
        )
        high = lax.ppermute(lax.slice_in_dim(block, 0, width, axis=dim), axis, backward)
        block = jnp.concatenate([low, block, high], axis=dim)
    return block


def shifted(value, axis, steps):
    count = lax.axis_size(axis)
    first, last = (max(0, -steps), min(count, count - steps))
    return lax.ppermute(value, axis, [(source, source + steps) for source in range(first, last)])


def activate(x_float, norm_gain):
    mean_sq = jnp.mean(x_float * x_float, axis=-1, keepdims=True)
    inv_rms = lax.rsqrt(mean_sq + epsilon)
    unit_val = x_float * inv_rms
    return (inv_rms, unit_val, unit_val * norm_gain)


def silu_slope(normed):
    sigma_val = jax.nn.sigmoid(normed)
    return sigma_val * (1.0 + normed * (1.0 - sigma_val))


def framed_cut(frames_x, strips, tile_cols):
    frame_count, height, width, channels = frames_x.shape
    padded = jnp.pad(frames_x, ((0, 0), (1, 1), (1, 1), (0, 0)))
    left_cols = padded[:, :, 0:width:tile_cols]
    mid_cols = padded[:, :, 1 : width + 1].reshape(
        frame_count, height + 2, strips, tile_cols, channels
    )
    right_cols = padded[:, :, tile_cols + 1 : width + 2 : tile_cols]
    framed = jnp.concatenate([left_cols[:, :, :, None], mid_cols, right_cols[:, :, :, None]], 3)
    return framed.transpose(2, 0, 1, 3, 4)


def spread(field):
    widened = extended_2(field, (("space", 2),), 1)
    return jnp.pad(widened, ((0, 0), (1, 1), (0, 0), (0, 0)))


def local(latents, norm_gain, conv_weight, skip_weight, cotangent):
    strips = lax.axis_size("space")
    frame_count, height, width, in_chan = latents.shape
    group_len, single, tile_rows, tile_cols, out_chan = cotangent.shape
    outgoing = framed_cut(latents, strips, tile_cols)
    arrived = lax.all_to_all(outgoing, "space", split_axis=0, concat_axis=1, tiled=True)[0]
    inv_pad, unit_pad, normed_pad = activate(arrived.astype(jnp.float32), norm_gain)
    hidden_pad = jax.nn.silu(normed_pad).astype(jnp.bfloat16)
    inv_rms = inv_pad[:, 1:-1, 1:-1]
    unit_val = unit_pad[:, 1:-1, 1:-1]
    normed = normed_pad[:, 1:-1, 1:-1]
    tile_x = arrived[:, 1:-1, 1:-1]
    past_rows = shifted(hidden_pad[group_len - 2 :], "tm", 1)
    extended = jnp.concatenate([past_rows, hidden_pad], 0)
    summed = jnp.dot(tile_x.reshape(-1, in_chan), skip_weight, preferred_element_type=jnp.float32)
    for t_tap in range(3):
        for h_tap in range(3):
            for w_tap in range(3):
                window = extended[
                    t_tap : t_tap + group_len, h_tap : h_tap + tile_rows, w_tap : w_tap + tile_cols
                ]
                summed = summed + jnp.dot(
                    window.reshape(-1, in_chan),
                    conv_weight[t_tap, h_tap, w_tap],
                    preferred_element_type=jnp.float32,
                )
    output = summed.astype(jnp.bfloat16).reshape(group_len, 1, tile_rows, tile_cols, out_chan)
    grad_out = cotangent[:, 0]
    grad_pad = spread(grad_out)
    next_rows = shifted(grad_pad[0:2], "tm", -1)
    grad_ext = jnp.concatenate([grad_pad, next_rows], 0)
    contract = (((1,), (1,)), ((), ()))
    grad_skip = lax.dot_general(
        grad_out.reshape(-1, out_chan), skip_weight, contract, preferred_element_type=jnp.float32
    )
    grad_hidden = jnp.zeros((group_len * tile_rows * tile_cols, in_chan), jnp.float32)
    for t_tap in range(3):
        for h_tap in range(3):
            for w_tap in range(3):
                window = grad_ext[
                    2 - t_tap : 2 - t_tap + group_len,
                    2 - h_tap : 2 - h_tap + tile_rows,
                    2 - w_tap : 2 - w_tap + tile_cols,
                ]
                grad_hidden = grad_hidden + lax.dot_general(
                    window.reshape(-1, out_chan),
                    conv_weight[t_tap, h_tap, w_tap],
                    contract,
                    preferred_element_type=jnp.float32,
                )
    grad_unit = (
        grad_hidden.reshape(group_len, tile_rows, tile_cols, in_chan)
        * silu_slope(normed)
        * norm_gain
    )
    grad_input = inv_rms * (
        grad_unit - unit_val * jnp.mean(grad_unit * unit_val, axis=-1, keepdims=True)
    )
    grad_input = grad_input + grad_skip.reshape(group_len, tile_rows, tile_cols, in_chan)
    return (
        output,
        grad_input.astype(jnp.bfloat16).reshape(group_len, 1, tile_rows, tile_cols, in_chan),
    )


def solution(mesh):
    placed = (
        P(("dp", "tm", "space"), None, None, None),
        P(),
        P(),
        P(),
        P(("dp", "tm"), "space", None, None, None),
    )
    return jax.shard_map(
        local,
        mesh=mesh,
        in_specs=placed,
        out_specs=(
            P(("dp", "tm"), "space", None, None, None),
            P(("dp", "tm"), "space", None, None, None),
        ),
        check_vma=False,
    )
```

profile of v0, /device:TPU:0, one launch (start us, length us, event | category | flops | bytes accessed | tf_op | source)
XLA Modules:
  0.0 74.0 jit_solution(17573924246514559045)
XLA Ops:
  0.7 1.1 %fusion.230 = (bf16[8,4,1,256]{3,2,1,0:T(2,128)(2,1)S(1)}, bf16[8,4,1,256]{3,2,1,0:T(2,128)(2,1)S(1)}) fusion(bf16[8,4,16,256]{3,2,1,0:T(8,128)(2,1)} %bitcast.283), kind=kLoop, calls=%fused_computation.333 | loop fusion | bytes 65536 | tf_op jit(solution)/shard_map/slice | solution.py:15
  1.7 2.4 %collective-permute-start.1 = (bf16[8,4,1,256]{3,2,1,0:T(2,128)(2,1)S(1)}, bf16[8,4,1,256]{3,2,1,0:T(2,128)(2,1)S(1)}, u32[]{:S(2)}, u32[]{:S(2)}) collective-permute-start(bf16[8,4,1,256]{3,2,1,0:T(2,128)(2,1)S(1)} %get-tuple-element.66), channel_id=1, source_target_pairs={{0,1},{1,2},{2,3},{3,4},{4,5},{5,6},{6,7},{8,9},{9,10},{10,11},{11... | collective-permute-start | bytes 49160 | tf_op jit(solution)/shard_map/ppermute | solution.py:14
  4.1 1.3 %collective-permute-start.2 = (bf16[8,4,1,256]{3,2,1,0:T(2,128)(2,1)S(1)}, bf16[8,4,1,256]{3,2,1,0:T(2,128)(2,1)S(1)}, u32[]{:S(2)}, u32[]{:S(2)}) collective-permute-start(bf16[8,4,1,256]{3,2,1,0:T(2,128)(2,1)S(1)} %get-tuple-element.67), channel_id=1, source_target_pairs={{1,0},{2,1},{3,2},{4,3},{5,4},{6,5},{7,6},{9,8},{10,9},{11,10},{12... | collective-permute-start | bytes 49160 | tf_op jit(solution)/shard_map/ppermute | solution.py:17
  5.4 1.2 %pad.8 = bf16[1,6,130,512]{3,2,1,0:T(8,128)(2,1)S(1)} pad(bf16[1,4,128,512]{3,2,1,0:T(8,128)(2,1)} %param.5, bf16[]{:T(256)} %constant.5.clone.1), padding=0_0x1_1x1_1x0_0 | pad | bytes 1323010 | tf_op jit(solution)/shard_map/jit(_pad)/pad | solution.py:42
  6.8 1.1 %pad_slice_fusion.68 = bf16[1,6,128,512]{3,2,1,0:T(8,128)(2,1)S(1)} fusion(bf16[1,4,128,512]{3,2,1,0:T(8,128)(2,1)} %param.5), kind=kLoop, calls=%fused_computation.325 | loop fusion | bytes 1310720 | tf_op jit(solution)/shard_map/slice | solution.py:44
  8.8 1.1 %copy.24 = bf16[8,1,6,18,512]{4,3,2,1,0:T(8,128)(2,1)} copy(bf16[8,1,6,18,512]{4,3,0,2,1:T(8,128)(2,1)S(1)} %maximum_bitcast_fusion) | data formatting | bytes 1769472 | tf_op jit(solution)/shard_map/transpose | solution.py:49
  10.0 8.5 %all-to-all-start = ((bf16[8,1,6,18,512]{4,3,2,1,0:T(8,128)(2,1)}), bf16[8,1,6,18,512]{4,3,2,1,0:T(8,128)(2,1)}, u32[]{:S(2)}, u32[]{:S(2)}) async-start(bf16[8,1,6,18,512]{4,3,2,1,0:T(8,128)(2,1)} %copy.24), calls=%async_computation | async-start | bytes 2359296 | tf_op jit(solution)/shard_map/all_to_all | solution.py:62
  18.4 1.3 %fusion.90 = f32[512,512]{1,0:T(8,128)S(1)} fusion(bf16[512,256]{1,0:T(8,128)(2,1)S(1)} %bitcast.284, bf16[3,3,3,512,256]{4,3,2,1,0:T(8,128)(2,1)} %param.7), kind=kOutput, calls=%fused_computation.189 | convolution fusion | flops 134217728 | bytes 1572864 | tf_op jit(solution)/shard_map/dot_general | solution.py:101
  20.2 1.3 %collective-permute-start.3 = (bf16[2,6,18,256]{3,2,1,0:T(8,128)(2,1)S(1)}, bf16[2,6,18,256]{3,2,1,0:T(8,128)(2,1)S(1)}, u32[]{:S(2)}, u32[]{:S(2)}) collective-permute-start(bf16[2,6,18,256]{3,2,1,0:T(8,128)(2,1)S(1)} %slice.445), channel_id=1, source_target_pairs={{8,0},{9,1},{10,2},{11,3},{12,4},{13,5},{14,6},{15,7},{24,16},{25,... | collective-permute-start | bytes 331784 | tf_op jit(solution)/shard_map/ppermute | solution.py:25
  21.6 1.4 %fusion.99 = f32[512,512]{1,0:T(8,128)S(1)} fusion(bf16[512,256]{1,0:T(8,128)(2,1)S(1)} %bitcast.340, bf16[3,3,3,512,256]{4,3,2,1,0:T(8,128)(2,1)} %param.7), kind=kOutput, calls=%fused_computation.198 | convolution fusion | flops 134217728 | bytes 1572864 | tf_op jit(solution)/shard_map/dot_general | solution.py:101
  23.0 1.3 %fusion.85 = f32[512,512]{1,0:T(8,128)S(1)} fusion(bf16[512,256]{1,0:T(8,128)(2,1)S(1)} %bitcast.339, bf16[3,3,3,512,256]{4,3,2,1,0:T(8,128)(2,1)} %param.7), kind=kOutput, calls=%fused_computation.184 | convolution fusion | flops 134217728 | bytes 1572864 | tf_op jit(solution)/shard_map/dot_general | solution.py:101
  24.5 3.9 %collective-permute-done.3 = bf16[2,6,18,256]{3,2,1,0:T(8,128)(2,1)S(1)} collective-permute-done((bf16[2,6,18,256]{3,2,1,0:T(8,128)(2,1)S(1)}, bf16[2,6,18,256]{3,2,1,0:T(8,128)(2,1)S(1)}, u32[]{:S(2)}, u32[]{:S(2)}) %collective-permute-start.3) | collective-permute-done | bytes 110624 | tf_op jit(solution)/shard_map/ppermute | solution.py:25
  34.8 1.7 %fusion.19 = f32[512,512]{1,0:T(8,128)S(1)} fusion(f32[512,512]{1,0:T(8,128)S(1)} %fusion.99, f32[512,512]{1,0:T(8,128)S(1)} %fusion.103, f32[512,512]{1,0:T(8,128)S(1)} %fusion.107, f32[512,512]{1,0:T(8,128)S(1)} %fusion.111, f32[512,512]{1,0:T(8,128)S(1)} %fusion.115, f32[512,512]{1,0:T(8,128)S(1)} %fusion.119, f32[512,512]{1,0:T(8,128)S(1)} %fusion.123, ...), kind=kOutput, calls=%fused_computation.66 | convolution fusion | flops 138936320 | bytes 20447232 | tf_op jit(solution)/shard_map/dot_general | solution.py:101
  38.2 1.3 %convolution_add_fusion.1 = f32[512,512]{1,0:T(8,128)} fusion(f32[512,512]{1,0:T(8,128)S(1)} %convolution_add_fusion.2, bf16[512,256]{1,0:T(8,128)(2,1)S(1)} %bitcast.319, bf16[3,3,3,512,256]{4,3,2,1,0:T(8,128)(2,1)S(1)} %bitcast.277), kind=kOutput, calls=%fused_computation.41 | convolution fusion | flops 134479872 | bytes 2621440 | tf_op jit(solution)/shard_map/dot_general | solution.py:101
  39.6 8.4 %all-to-all-done = bf16[8,1,6,18,512]{4,3,2,1,0:T(8,128)(2,1)} async-done(((bf16[8,1,6,18,512]{4,3,2,1,0:T(8,128)(2,1)}), bf16[8,1,6,18,512]{4,3,2,1,0:T(8,128)(2,1)}, u32[]{:S(2)}, u32[]{:S(2)}) %all-to-all-start) | async-done | bytes 884768 | tf_op jit(solution)/shard_map/all_to_all | solution.py:62
  47.9 1.6 %fusion = f32[8,6,18]{2,1,0:T(8,128)S(1)} fusion(bf16[8,1,6,18,512]{4,3,2,1,0:T(8,128)(2,1)} %all-to-all-done), kind=kLoop, calls=%fused_computation.36 | loop fusion | flops 1326240 | bytes 888192 | tf_op jit(solution)/shard_map/reduce_sum | solution.py:29
  49.6 2.1 %broadcast_multiply_fusion = (f32[8,6,18,512]{3,2,1,0:T(8,128)S(1)}, bf16[8,6,18,512]{3,2,1,0:T(8,128)(2,1)S(1)}, f32[8,6,18,512]{3,2,1,0:T(8,128)S(1)}) fusion(f32[512]{0:T(512)S(1)} %copy-done.3, f32[8,6,18]{2,1,0:T(8,128)S(1)} %get-tuple-element.69, bf16[8,1,6,18,512]{4,3,2,1,0:T(8,128)(2,1)} %all-to-all-done), kind=kLoop, calls=%fused_computation.98 | loop fusion | flops 3538944 | bytes 5313920 | tf_op jit(solution)/shard_map/mul | solution.py:32
  53.1 3.7 %collective-permute-start = (bf16[2,6,18,512]{3,2,1,0:T(8,128)(2,1)S(1)}, bf16[2,6,18,512]{3,2,1,0:T(8,128)(2,1)S(1)}, u32[]{:S(2)}, u32[]{:S(2)}) collective-permute-start(bf16[2,6,18,512]{3,2,1,0:T(8,128)(2,1)S(1)} %slice.398), channel_id=1, source_target_pairs={{0,8},{1,9},{2,10},{3,11},{4,12},{5,13},{6,14},{7,15},{16,24},{17,... | collective-permute-start | bytes 663560 | tf_op jit(solution)/shard_map/ppermute | solution.py:25
  56.8 1.3 %slice.397 = bf16[8,4,16,512]{3,2,1,0:T(8,128)(2,1)S(1)} slice(bf16[8,6,18,512]{3,2,1,0:T(8,128)(2,1)} %bitcast.4), slice={[0:8], [1:5], [1:17], [0:512]} | slice | bytes 1048576 | tf_op jit(solution)/shard_map/slice | solution.py:68
  58.5 1.6 %fusion.21 = bf16[8,1,4,16,512]{4,3,2,1,0:T(8,128)(2,1)} fusion(f32[8,6,18,512]{3,2,1,0:T(8,128)S(1)} %get-tuple-element.30, f32[8,4,16]{2,1,0:T(4,128)S(1)} %broadcast_multiply_fusion.1, f32[8,4,16]{2,1,0:T(4,128)S(1)} %slice_bitcast_fusion, bf16[512,256]{1,0:T(8,128)(2,1)S(1)} %copy-done, bf16[8,1,4,16,256]{4,3,2,1,0:T(8,128)(2,1)S(1)} %copy-done.2, ...), kind=kOutput, calls=%fused_computation.68 | convolution fusion | flops 137887744 | bytes 4200448 | tf_op jit(solution)/shard_map/dot_general | solution.py:89
  60.6 2.0 %collective-permute-done = bf16[2,6,18,512]{3,2,1,0:T(8,128)(2,1)S(1)} collective-permute-done((bf16[2,6,18,512]{3,2,1,0:T(8,128)(2,1)S(1)}, bf16[2,6,18,512]{3,2,1,0:T(8,128)(2,1)S(1)}, u32[]{:S(2)}, u32[]{:S(2)}) %collective-permute-start) | collective-permute-done | bytes 221216 | tf_op jit(solution)/shard_map/ppermute | solution.py:25
  62.6 1.1 %fusion.48 = (bf16[8,4,16,512]{3,2,1,0:T(8,128)(2,1)S(1)}, bf16[8,4,16,512]{3,2,1,0:T(8,128)(2,1)S(1)}, bf16[8,4,16,512]{3,2,1,0:T(8,128)(2,1)S(1)}, bf16[8,4,16...) fusion(bf16[8,6,18,512]{3,2,1,0:T(8,128)(2,1)S(1)} %get-tuple-e, ...), kind=kLoop, calls=%fused_computation.126 | loop fusion | flops 2359296 | bytes 7241728 | tf_op jit(solution)/shard_map/concatenate | solution.py:70
  65.8 1.3 %fusion.56 = (bf16[8,4,16,512]{3,2,1,0:T(8,128)(2,1)S(1)}, bf16[8,4,16,512]{3,2,1,0:T(8,128)(2,1)S(1)}, bf16[8,4,16,512]{3,2,1,0:T(8,128)(2,1)S(1)}, bf16[8,4,16...) fusion(bf16[8,6,18,512]{3,2,1,0:T(8,128)(2,1)S(1)} %get-tuple-e, ...), kind=kLoop, calls=%fused_computation.134 | loop fusion | flops 9437184 | bytes 7241728 | tf_op jit(solution)/shard_map/concatenate | solution.py:70
  73.0 1.0 %fusion.39 = bf16[512,256]{1,0:T(8,128)(2,1)} fusion(f32[512,256]{1,0:T(8,128)S(1)} %convolution_add_fusion.9, bf16[512,512]{1,0:T(8,128)(2,1)S(1)} %bitcast.294, bf16[3,3,3,512,256]{4,3,2,1,0:T(8,128)(2,1)S(1)} %bitcast.279), kind=kOutput, calls=%fused_computation.96 | convolution fusion | flops 134479872 | bytes 1572864 | tf_op jit(solution)/shard_map/dot_general | solution.py:78
  (86 shorter events, 19.6 us)
Async XLA Ops:
  0.6 57.5 %copy-start = (bf16[512,256]{1,0:T(8,128)(2,1)S(1)}, bf16[512,256]{1,0:T(8,128)(2,1)}, u32[]{:S(2)}) copy-start(bf16[512,256]{1,0:T(8,128)(2,1)} %param.8) | copy-start | bytes 786436
  0.6 17.8 %copy-start.2 = (bf16[8,1,4,16,256]{4,3,2,1,0:T(8,128)(2,1)S(1)}, bf16[8,1,4,16,256]{4,3,2,1,0:T(8,128)(2,1)}, u32[]{:S(2)}) copy-start(bf16[8,1,4,16,256]{4,3,2,1,0:T(8,128)(2,1)} %param.9) | copy-start | bytes 786436
  1.7 18.0 %collective-permute-start.1 = (bf16[8,4,1,256]{3,2,1,0:T(2,128)(2,1)S(1)}, bf16[8,4,1,256]{3,2,1,0:T(2,128)(2,1)S(1)}, u32[]{:S(2)}, u32[]{:S(2)}) collective-permute-start(bf16[8,4,1,256]{3,2,1,0:T(2,128)(2,1)S(1)} %get-tuple-element.66), channel_id=1, source_target_pairs={{0,1},{1,2},{2,3},{3,4},{4,5},{5,6},{6,7},{8,9},{9,10},{10,11},{11... | collective-permute-start | bytes 49160 | tf_op jit(solution)/shard_map/ppermute | solution.py:14
  4.1 15.6 %collective-permute-start.2 = (bf16[8,4,1,256]{3,2,1,0:T(2,128)(2,1)S(1)}, bf16[8,4,1,256]{3,2,1,0:T(2,128)(2,1)S(1)}, u32[]{:S(2)}, u32[]{:S(2)}) collective-permute-start(bf16[8,4,1,256]{3,2,1,0:T(2,128)(2,1)S(1)} %get-tuple-element.67), channel_id=1, source_target_pairs={{1,0},{2,1},{3,2},{4,3},{5,4},{6,5},{7,6},{9,8},{10,9},{11,10},{12... | collective-permute-start | bytes 49160 | tf_op jit(solution)/shard_map/ppermute | solution.py:17
  10.0 18.9 %slice-start = ((s8[7077888]{0:T(1024)(128)(4,1)}), s8[2883584]{0:T(1024)(128)(4,1)S(1)}, s32[]{:S(2)}) async-start(s8[7077888]{0:T(1024)(128)(4,1)} %bitcast.276), calls=%async_computation.1 | async-start | bytes 5767168
  10.0 38.0 %all-to-all-start = ((bf16[8,1,6,18,512]{4,3,2,1,0:T(8,128)(2,1)}), bf16[8,1,6,18,512]{4,3,2,1,0:T(8,128)(2,1)}, u32[]{:S(2)}, u32[]{:S(2)}) async-start(bf16[8,1,6,18,512]{4,3,2,1,0:T(8,128)(2,1)} %copy.24), calls=%async_computation | async-start | bytes 2359296 | tf_op jit(solution)/shard_map/all_to_all | solution.py:62
  20.2 8.2 %collective-permute-start.3 = (bf16[2,6,18,256]{3,2,1,0:T(8,128)(2,1)S(1)}, bf16[2,6,18,256]{3,2,1,0:T(8,128)(2,1)S(1)}, u32[]{:S(2)}, u32[]{:S(2)}) collective-permute-start(bf16[2,6,18,256]{3,2,1,0:T(8,128)(2,1)S(1)} %slice.445), channel_id=1, source_target_pairs={{8,0},{9,1},{10,2},{11,3},{12,4},{13,5},{14,6},{15,7},{24,16},{25,... | collective-permute-start | bytes 331784 | tf_op jit(solution)/shard_map/ppermute | solution.py:25
  21.5 7.4 %slice-start.1 = ((s8[7077888]{0:T(1024)(128)(4,1)}), s8[4194304]{0:T(1024)(128)(4,1)S(1)}, s32[]{:S(2)}) async-start(s8[7077888]{0:T(1024)(128)(4,1)} %bitcast.276), calls=%async_computation.2 | async-start | bytes 8388608
  37.1 12.4 %copy-start.3 = (f32[512]{0:T(512)S(1)}, f32[512]{0:T(512)}, u32[]{:S(2)}) copy-start(f32[512]{0:T(512)} %param.6) | copy-start | bytes 6148
  49.6 2.8 %copy-start.1 = (f32[512,512]{1,0:T(8,128)S(1)}, f32[512,512]{1,0:T(8,128)}, u32[]{:S(2)}) copy-start(f32[512,512]{1,0:T(8,128)} %convolution_add_fusion.1) | copy-start | bytes 3145732
  52.3 7.8 %slice-start.2 = ((s8[7077888]{0:T(1024)(128)(4,1)}), s8[4194304]{0:T(1024)(128)(4,1)S(1)}, s32[]{:S(2)}) async-start(s8[7077888]{0:T(1024)(128)(4,1)} %bitcast.278), calls=%async_computation.3 | async-start | bytes 8388608
  53.1 9.5 %collective-permute-start = (bf16[2,6,18,512]{3,2,1,0:T(8,128)(2,1)S(1)}, bf16[2,6,18,512]{3,2,1,0:T(8,128)(2,1)S(1)}, u32[]{:S(2)}, u32[]{:S(2)}) collective-permute-start(bf16[2,6,18,512]{3,2,1,0:T(8,128)(2,1)S(1)} %slice.398), channel_id=1, source_target_pairs={{0,8},{1,9},{2,10},{3,11},{4,12},{5,13},{6,14},{7,15},{16,24},{17,... | collective-permute-start | bytes 663560 | tf_op jit(solution)/shard_map/ppermute | solution.py:25
  58.4 1.8 %slice-start.3 = ((s8[7077888]{0:T(1024)(128)(4,1)}), s8[2883584]{0:T(1024)(128)(4,1)S(1)}, s32[]{:S(2)}) async-start(s8[7077888]{0:T(1024)(128)(4,1)} %bitcast.278), calls=%async_computation.4 | async-start | bytes 5767168
where the time goes:
time: 74.5 us; the launch traced here: 74 us
  matrix products  25.2 us (34%)
  starting transfers between devices  17.2 us (23%)
  waiting for transfers between devices  14.3 us (19%)
  other arithmetic  8.74 us (12%)
  local copies, waits for them, and re-layouts  7.31 us (10%)
  between operations  1.28 us (2%)
    dot_general x27, matrix products, local(): lax.dot_general(window.reshape(-1, out_chan), conv_weight[t_tap, h_tap, w...  14.2 us
    dot_general x27, matrix products, local(): jnp.dot(window.reshape(-1, in_chan), conv_weight[t_tap, h_tap, w_tap], pr...  9 us
    all_to_all x1, starting transfers between devices, local(): lax.all_to_all(outgoing, 'space', split_axis=0, concat_axis=1, tiled=True)  8.49 us
    all_to_all x1, waiting for transfers between devices, local(): lax.all_to_all(outgoing, 'space', split_axis=0, concat_axis=1, tiled=True)  8.37 us
    ppermute x2, waiting for transfers between devices, shifted(): lax.ppermute(value, axis, [(source, source + steps) for source in range(f...  5.89 us
    ppermute x2, starting transfers between devices, shifted(): lax.ppermute(value, axis, [(source, source + steps) for source in range(f...  5.04 us
    concatenate x2, other arithmetic, local(): extended = jnp.concatenate([past_rows, hidden_pad], 0)  2.48 us
    ppermute x1, starting transfers between devices, extended_2(): lax.ppermute(lax.slice_in_dim(block, block.shape[dim] - width, None, axis...  2.4 us
  transfers between devices with their start and end apart: 5, of which 3 were waited for; matrix products, arithmetic and copies ran while one was open for 32% of the time, Pallas kernels for 0%

commit v1 on v0

--- a/solution.py
+++ b/solution.py
@@ -59,7 +59,12 @@
     frame_count, height, width, in_chan = latents.shape
     group_len, single, tile_rows, tile_cols, out_chan = cotangent.shape
     outgoing = framed_cut(latents, strips, tile_cols)
-    arrived = lax.all_to_all(outgoing, "space", split_axis=0, concat_axis=1, tiled=True)[0]
+    arrived = jnp.concatenate(
+        lax.all_to_all(
+            jnp.stack(jnp.split(outgoing, lax.axis_size("space"), axis=0)), "space", 0, 0
+        ),
+        axis=1,
+    )[0]
     inv_pad, unit_pad, normed_pad = activate(arrived.astype(jnp.float32), norm_gain)
     hidden_pad = jax.nn.silu(normed_pad).astype(jnp.bfloat16)
     inv_rms = inv_pad[:, 1:-1, 1:-1]

time: 74.5 us -> 79.2 us (1.063)
  local copies, waits for them, and re-layouts: 7.31 us -> 12.2 us
    unnamed x16 -> x23, local copies, waits for them, and re-layouts: 0.22 us -> 5.63 us
    transpose x1 -> x0, local copies, waits for them, and re-layouts: 1.13 us -> none  [framed_cut(): return framed.transpose(2, 0, 1, 3, 4)]
  transfers between devices with their start and end apart: 5 -> 5, of which waited for: 3 -> 3; matrix products, arithmetic and copies ran while one was open for 32% -> 35% of each run, Pallas kernels for 0% -> 0%
where the time goes in v1:
time: 79.2 us; the launch traced here: 78.7 us
  matrix products  25.3 us (32%)
  starting transfers between devices  17.2 us (22%)
  waiting for transfers between devices  14.1 us (18%)
  local copies, waits for them, and re-layouts  12.2 us (15%)
  other arithmetic  8.51 us (11%)
  between operations  1.27 us (2%)
    dot_general x27, matrix products, local(): lax.dot_general(window.reshape(-1, out_chan), conv_weight[t_tap, h_tap, w...  14.2 us
    dot_general x27, matrix products, local(): jnp.dot(window.reshape(-1, in_chan), conv_weight[t_tap, h_tap, w_tap], pr...  9.16 us
    all_to_all x1, starting transfers between devices, local(): lax.all_to_all(jnp.stack(jnp.split(outgoing, lax.axis_size('space'), axis...  8.49 us
    all_to_all x1, waiting for transfers between devices, local(): lax.all_to_all(jnp.stack(jnp.split(outgoing, lax.axis_size('space'), axis...  8.37 us
    ppermute x2, waiting for transfers between devices, shifted(): lax.ppermute(value, axis, [(source, source + steps) for source in range(f...  5.77 us
    unnamed x23, local copies, waits for them, and re-layouts  5.63 us
    ppermute x2, starting transfers between devices, shifted(): lax.ppermute(value, axis, [(source, source + steps) for source in range(f...  5.04 us
    ppermute x1, starting transfers between devices, extended_2(): lax.ppermute(lax.slice_in_dim(block, block.shape[dim] - width, None, axis...  2.4 us
  transfers between devices with their start and end apart: 5, of which 3 were waited for; matrix products, arithmetic and copies ran while one was open for 35% of the time, Pallas kernels for 0%

profile of v1, /device:TPU:0, one launch (start us, length us, event | category | flops | bytes accessed | tf_op | source)
XLA Modules:
  0.0 78.7 jit_solution(3330312876080209239)
XLA Ops:
  0.6 1.1 %fusion.238 = (bf16[8,4,1,256]{3,2,1,0:T(2,128)(2,1)S(1)}, bf16[8,4,1,256]{3,2,1,0:T(2,128)(2,1)S(1)}) fusion(bf16[8,4,16,256]{3,2,1,0:T(8,128)(2,1)} %bitcast.329), kind=kLoop, calls=%fused_computation.349 | loop fusion | bytes 65536 | tf_op jit(solution)/shard_map/slice | solution.py:15
  1.7 2.4 %collective-permute-start.1 = (bf16[8,4,1,256]{3,2,1,0:T(2,128)(2,1)S(1)}, bf16[8,4,1,256]{3,2,1,0:T(2,128)(2,1)S(1)}, u32[]{:S(2)}, u32[]{:S(2)}) collective-permute-start(bf16[8,4,1,256]{3,2,1,0:T(2,128)(2,1)S(1)} %get-tuple-element.66), channel_id=1, source_target_pairs={{0,1},{1,2},{2,3},{3,4},{4,5},{5,6},{6,7},{8,9},{9,10},{10,11},{11... | collective-permute-start | bytes 49160 | tf_op jit(solution)/shard_map/ppermute | solution.py:14
  4.1 1.3 %collective-permute-start.2 = (bf16[8,4,1,256]{3,2,1,0:T(2,128)(2,1)S(1)}, bf16[8,4,1,256]{3,2,1,0:T(2,128)(2,1)S(1)}, u32[]{:S(2)}, u32[]{:S(2)}) collective-permute-start(bf16[8,4,1,256]{3,2,1,0:T(2,128)(2,1)S(1)} %get-tuple-element.67), channel_id=1, source_target_pairs={{1,0},{2,1},{3,2},{4,3},{5,4},{6,5},{7,6},{9,8},{10,9},{11,10},{12... | collective-permute-start | bytes 49160 | tf_op jit(solution)/shard_map/ppermute | solution.py:17
  5.4 1.2 %pad.8 = bf16[1,6,130,512]{3,2,1,0:T(8,128)(2,1)S(1)} pad(bf16[1,4,128,512]{3,2,1,0:T(8,128)(2,1)} %param.5, bf16[]{:T(256)} %constant.5.clone.1), padding=0_0x1_1x1_1x0_0 | pad | bytes 1323010 | tf_op jit(solution)/shard_map/jit(_pad)/pad | solution.py:42
  6.8 1.1 %pad_slice_fusion.68 = bf16[1,6,128,512]{3,2,1,0:T(8,128)(2,1)S(1)} fusion(bf16[1,4,128,512]{3,2,1,0:T(8,128)(2,1)} %param.5), kind=kLoop, calls=%fused_computation.341 | loop fusion | bytes 1310720 | tf_op jit(solution)/shard_map/slice | solution.py:44
  14.1 8.5 %all-to-all-start = ((bf16[8,1,1,6,18,512]{5,4,3,2,1,0:T(8,128)(2,1)}), bf16[8,1,1,6,18,512]{5,4,3,2,1,0:T(8,128)(2,1)}, u32[]{:S(2)}, u32[]{:S(2)}) async-start(bf16[8,1,1,6,18,512]{5,4,3,2,1,0:T(8,128)(2,1)} %fusion.226), calls=%async_computation | async-start | bytes 2359296 | tf_op jit(solution)/shard_map/all_to_all | solution.py:63
  22.6 1.3 %fusion.90 = f32[512,512]{1,0:T(8,128)S(1)} fusion(bf16[512,256]{1,0:T(8,128)(2,1)S(1)} %bitcast.330, bf16[3,3,3,512,256]{4,3,2,1,0:T(8,128)(2,1)} %param.7), kind=kOutput, calls=%fused_computation.189 | convolution fusion | flops 134217728 | bytes 1572864 | tf_op jit(solution)/shard_map/dot_general | solution.py:106
  24.4 1.3 %collective-permute-start.3 = (bf16[2,6,18,256]{3,2,1,0:T(8,128)(2,1)S(1)}, bf16[2,6,18,256]{3,2,1,0:T(8,128)(2,1)S(1)}, u32[]{:S(2)}, u32[]{:S(2)}) collective-permute-start(bf16[2,6,18,256]{3,2,1,0:T(8,128)(2,1)S(1)} %slice.445), channel_id=1, source_target_pairs={{8,0},{9,1},{10,2},{11,3},{12,4},{13,5},{14,6},{15,7},{24,16},{25,... | collective-permute-start | bytes 331784 | tf_op jit(solution)/shard_map/ppermute | solution.py:25
  25.7 1.4 %fusion.99 = f32[512,512]{1,0:T(8,128)S(1)} fusion(bf16[512,256]{1,0:T(8,128)(2,1)S(1)} %bitcast.386, bf16[3,3,3,512,256]{4,3,2,1,0:T(8,128)(2,1)} %param.7), kind=kOutput, calls=%fused_computation.198 | convolution fusion | flops 134217728 | bytes 1572864 | tf_op jit(solution)/shard_map/dot_general | solution.py:106
  27.2 1.3 %fusion.85 = f32[512,512]{1,0:T(8,128)S(1)} fusion(bf16[512,256]{1,0:T(8,128)(2,1)S(1)} %bitcast.385, bf16[3,3,3,512,256]{4,3,2,1,0:T(8,128)(2,1)} %param.7), kind=kOutput, calls=%fused_computation.184 | convolution fusion | flops 134217728 | bytes 1572864 | tf_op jit(solution)/shard_map/dot_general | solution.py:106
  28.7 3.9 %collective-permute-done.3 = bf16[2,6,18,256]{3,2,1,0:T(8,128)(2,1)S(1)} collective-permute-done((bf16[2,6,18,256]{3,2,1,0:T(8,128)(2,1)S(1)}, bf16[2,6,18,256]{3,2,1,0:T(8,128)(2,1)S(1)}, u32[]{:S(2)}, u32[]{:S(2)}) %collective-permute-start.3) | collective-permute-done | bytes 110624 | tf_op jit(solution)/shard_map/ppermute | solution.py:25
  39.0 1.7 %fusion.19 = f32[512,512]{1,0:T(8,128)S(1)} fusion(f32[512,512]{1,0:T(8,128)S(1)} %fusion.99, f32[512,512]{1,0:T(8,128)S(1)} %fusion.103, f32[512,512]{1,0:T(8,128)S(1)} %fusion.107, f32[512,512]{1,0:T(8,128)S(1)} %fusion.111, f32[512,512]{1,0:T(8,128)S(1)} %fusion.115, f32[512,512]{1,0:T(8,128)S(1)} %fusion.119, f32[512,512]{1,0:T(8,128)S(1)} %fusion.123, ...), kind=kOutput, calls=%fused_computation.66 | convolution fusion | flops 138936320 | bytes 20447232 | tf_op jit(solution)/shard_map/dot_general | solution.py:106
  42.4 1.3 %convolution_add_fusion.1 = f32[512,512]{1,0:T(8,128)} fusion(f32[512,512]{1,0:T(8,128)S(1)} %convolution_add_fusion.2, bf16[512,256]{1,0:T(8,128)(2,1)S(1)} %bitcast.365, bf16[3,3,3,512,256]{4,3,2,1,0:T(8,128)(2,1)S(1)} %bitcast.323), kind=kOutput, calls=%fused_computation.41 | convolution fusion | flops 134479872 | bytes 2621440 | tf_op jit(solution)/shard_map/dot_general | solution.py:106
  43.7 8.4 %all-to-all-done = bf16[8,1,1,6,18,512]{5,4,3,2,1,0:T(8,128)(2,1)} async-done(((bf16[8,1,1,6,18,512]{5,4,3,2,1,0:T(8,128)(2,1)}), bf16[8,1,1,6,18,512]{5,4,3,2,1,0:T(8,128)(2,1)}, u32[]{:S(2)}, u32[]{:S(2)}) %all-to-all-start) | async-done | bytes 884768 | tf_op jit(solution)/shard_map/all_to_all | solution.py:63
  52.1 1.6 %fusion = f32[8,6,18]{2,1,0:T(8,128)S(1)} fusion(bf16[8,1,1,6,18,512]{5,4,3,2,1,0:T(8,128)(2,1)} %all-to-all-done), kind=kLoop, calls=%fused_computation.36 | loop fusion | flops 1326240 | bytes 888192 | tf_op jit(solution)/shard_map/reduce_sum | solution.py:29
  53.7 2.0 %broadcast_multiply_fusion = (f32[8,6,18,512]{3,2,1,0:T(8,128)S(1)}, bf16[8,6,18,512]{3,2,1,0:T(8,128)(2,1)S(1)}, f32[8,6,18,512]{3,2,1,0:T(8,128)S(1)}) fusion(f32[512]{0:T(512)S(1)} %copy-done.3, f32[8,6,18]{2,1,0:T(8,128)S(1)} %get-tuple-element.69, bf16[8,1,1,6,18,512]{5,4,3,2,1,0:T(8,128)(2,1)} %all-to-all-done), kind=kLoop, calls=%fused_computation.98 | loop fusion | flops 3538944 | bytes 5313920 | tf_op jit(solution)/shard_map/mul | solution.py:32
  57.7 3.7 %collective-permute-start = (bf16[2,6,18,512]{3,2,1,0:T(8,128)(2,1)S(1)}, bf16[2,6,18,512]{3,2,1,0:T(8,128)(2,1)S(1)}, u32[]{:S(2)}, u32[]{:S(2)}) collective-permute-start(bf16[2,6,18,512]{3,2,1,0:T(8,128)(2,1)S(1)} %slice.398), channel_id=1, source_target_pairs={{0,8},{1,9},{2,10},{3,11},{4,12},{5,13},{6,14},{7,15},{16,24},{17,... | collective-permute-start | bytes 663560 | tf_op jit(solution)/shard_map/ppermute | solution.py:25
  61.5 1.3 %slice.397 = bf16[8,4,16,512]{3,2,1,0:T(8,128)(2,1)S(1)} slice(bf16[8,6,18,512]{3,2,1,0:T(8,128)(2,1)} %bitcast.12), slice={[0:8], [1:5], [1:17], [0:512]} | slice | bytes 1048576 | tf_op jit(solution)/shard_map/slice | solution.py:73
  63.1 1.6 %fusion.21 = bf16[8,1,4,16,512]{4,3,2,1,0:T(8,128)(2,1)} fusion(f32[8,6,18,512]{3,2,1,0:T(8,128)S(1)} %get-tuple-element.30, f32[8,4,16]{2,1,0:T(4,128)S(1)} %broadcast_multiply_fusion.1, f32[8,4,16]{2,1,0:T(4,128)S(1)} %slice_bitcast_fusion.8, bf16[512,256]{1,0:T(8,128)(2,1)S(1)} %copy-done, bf16[8,1,4,16,256]{4,3,2,1,0:T(8,128)(2,1)S(1)} %copy-done.2, ...), kind=kOutput, calls=%fused_computation.68 | convolution fusion | flops 137887744 | bytes 4200448 | tf_op jit(solution)/shard_map/dot_general | solution.py:94
  65.3 1.9 %collective-permute-done = bf16[2,6,18,512]{3,2,1,0:T(8,128)(2,1)S(1)} collective-permute-done((bf16[2,6,18,512]{3,2,1,0:T(8,128)(2,1)S(1)}, bf16[2,6,18,512]{3,2,1,0:T(8,128)(2,1)S(1)}, u32[]{:S(2)}, u32[]{:S(2)}) %collective-permute-start) | collective-permute-done | bytes 221216 | tf_op jit(solution)/shard_map/ppermute | solution.py:25
  67.2 1.1 %fusion.48 = (bf16[8,4,16,512]{3,2,1,0:T(8,128)(2,1)S(1)}, bf16[8,4,16,512]{3,2,1,0:T(8,128)(2,1)S(1)}, bf16[8,4,16,512]{3,2,1,0:T(8,128)(2,1)S(1)}, bf16[8,4,16...) fusion(bf16[8,6,18,512]{3,2,1,0:T(8,128)(2,1)S(1)} %get-tuple-e, ...), kind=kLoop, calls=%fused_computation.126 | loop fusion | flops 2359296 | bytes 7241728 | tf_op jit(solution)/shard_map/concatenate | solution.py:75
  70.5 1.3 %fusion.56 = (bf16[8,4,16,512]{3,2,1,0:T(8,128)(2,1)S(1)}, bf16[8,4,16,512]{3,2,1,0:T(8,128)(2,1)S(1)}, bf16[8,4,16,512]{3,2,1,0:T(8,128)(2,1)S(1)}, bf16[8,4,16...) fusion(bf16[8,6,18,512]{3,2,1,0:T(8,128)(2,1)S(1)} %get-tuple-e, ...), kind=kLoop, calls=%fused_computation.134 | loop fusion | flops 9437184 | bytes 7241728 | tf_op jit(solution)/shard_map/concatenate | solution.py:75
  74.7 0.8 fusion.38
  77.7 1.0 %fusion.39 = bf16[512,256]{1,0:T(8,128)(2,1)} fusion(f32[512,256]{1,0:T(8,128)S(1)} %convolution_add_fusion.9, bf16[512,512]{1,0:T(8,128)(2,1)S(1)} %bitcast.340, bf16[3,3,3,512,256]{4,3,2,1,0:T(8,128)(2,1)S(1)} %bitcast.325), kind=kOutput, calls=%fused_computation.96 | convolution fusion | flops 134479872 | bytes 1572864 | tf_op jit(solution)/shard_map/dot_general | solution.py:83
  (93 shorter events, 25.1 us)
Async XLA Ops:
  0.6 62.2 %copy-start = (bf16[512,256]{1,0:T(8,128)(2,1)S(1)}, bf16[512,256]{1,0:T(8,128)(2,1)}, u32[]{:S(2)}) copy-start(bf16[512,256]{1,0:T(8,128)(2,1)} %param.8) | copy-start | bytes 786436
  1.7 22.2 %collective-permute-start.1 = (bf16[8,4,1,256]{3,2,1,0:T(2,128)(2,1)S(1)}, bf16[8,4,1,256]{3,2,1,0:T(2,128)(2,1)S(1)}, u32[]{:S(2)}, u32[]{:S(2)}) collective-permute-start(bf16[8,4,1,256]{3,2,1,0:T(2,128)(2,1)S(1)} %get-tuple-element.66), channel_id=1, source_target_pairs={{0,1},{1,2},{2,3},{3,4},{4,5},{5,6},{6,7},{8,9},{9,10},{10,11},{11... | collective-permute-start | bytes 49160 | tf_op jit(solution)/shard_map/ppermute | solution.py:14
  4.1 19.8 %collective-permute-start.2 = (bf16[8,4,1,256]{3,2,1,0:T(2,128)(2,1)S(1)}, bf16[8,4,1,256]{3,2,1,0:T(2,128)(2,1)S(1)}, u32[]{:S(2)}, u32[]{:S(2)}) collective-permute-start(bf16[8,4,1,256]{3,2,1,0:T(2,128)(2,1)S(1)} %get-tuple-element.67), channel_id=1, source_target_pairs={{1,0},{2,1},{3,2},{4,3},{5,4},{6,5},{7,6},{9,8},{10,9},{11,10},{12... | collective-permute-start | bytes 49160 | tf_op jit(solution)/shard_map/ppermute | solution.py:17
  8.8 13.8 %copy-start.2 = (bf16[8,1,4,16,256]{4,3,2,1,0:T(8,128)(2,1)S(1)}, bf16[8,1,4,16,256]{4,3,2,1,0:T(8,128)(2,1)}, u32[]{:S(2)}) copy-start(bf16[8,1,4,16,256]{4,3,2,1,0:T(8,128)(2,1)} %param.9) | copy-start | bytes 786436
  14.1 18.9 %slice-start = ((s8[7077888]{0:T(1024)(128)(4,1)}), s8[2883584]{0:T(1024)(128)(4,1)S(1)}, s32[]{:S(2)}) async-start(s8[7077888]{0:T(1024)(128)(4,1)} %bitcast.322), calls=%async_computation.1 | async-start | bytes 5767168
  14.1 38.0 %all-to-all-start = ((bf16[8,1,1,6,18,512]{5,4,3,2,1,0:T(8,128)(2,1)}), bf16[8,1,1,6,18,512]{5,4,3,2,1,0:T(8,128)(2,1)}, u32[]{:S(2)}, u32[]{:S(2)}) async-start(bf16[8,1,1,6,18,512]{5,4,3,2,1,0:T(8,128)(2,1)} %fusion.226), calls=%async_computation | async-start | bytes 2359296 | tf_op jit(solution)/shard_map/all_to_all | solution.py:63
  24.4 8.2 %collective-permute-start.3 = (bf16[2,6,18,256]{3,2,1,0:T(8,128)(2,1)S(1)}, bf16[2,6,18,256]{3,2,1,0:T(8,128)(2,1)S(1)}, u32[]{:S(2)}, u32[]{:S(2)}) collective-permute-start(bf16[2,6,18,256]{3,2,1,0:T(8,128)(2,1)S(1)} %slice.445), channel_id=1, source_target_pairs={{8,0},{9,1},{10,2},{11,3},{12,4},{13,5},{14,6},{15,7},{24,16},{25,... | collective-permute-start | bytes 331784 | tf_op jit(solution)/shard_map/ppermute | solution.py:25
  25.7 7.4 %slice-start.1 = ((s8[7077888]{0:T(1024)(128)(4,1)}), s8[4194304]{0:T(1024)(128)(4,1)S(1)}, s32[]{:S(2)}) async-start(s8[7077888]{0:T(1024)(128)(4,1)} %bitcast.322), calls=%async_computation.2 | async-start | bytes 8388608
  42.4 11.3 %copy-start.3 = (f32[512]{0:T(512)S(1)}, f32[512]{0:T(512)}, u32[]{:S(2)}) copy-start(f32[512]{0:T(512)} %param.6) | copy-start | bytes 6148
  55.8 1.2 %copy-start.1 = (f32[512,512]{1,0:T(8,128)S(1)}, f32[512,512]{1,0:T(8,128)}, u32[]{:S(2)}) copy-start(f32[512,512]{1,0:T(8,128)} %convolution_add_fusion.1) | copy-start | bytes 3145732
  57.0 7.7 %slice-start.2 = ((s8[7077888]{0:T(1024)(128)(4,1)}), s8[4194304]{0:T(1024)(128)(4,1)S(1)}, s32[]{:S(2)}) async-start(s8[7077888]{0:T(1024)(128)(4,1)} %bitcast.324), calls=%async_computation.3 | async-start | bytes 8388608
  57.7 9.5 %collective-permute-start = (bf16[2,6,18,512]{3,2,1,0:T(8,128)(2,1)S(1)}, bf16[2,6,18,512]{3,2,1,0:T(8,128)(2,1)S(1)}, u32[]{:S(2)}, u32[]{:S(2)}) collective-permute-start(bf16[2,6,18,512]{3,2,1,0:T(8,128)(2,1)S(1)} %slice.398), channel_id=1, source_target_pairs={{0,8},{1,9},{2,10},{3,11},{4,12},{5,13},{6,14},{7,15},{16,24},{17,... | collective-permute-start | bytes 663560 | tf_op jit(solution)/shard_map/ppermute | solution.py:25
  63.1 1.9 %slice-start.3 = ((s8[7077888]{0:T(1024)(128)(4,1)}), s8[2883584]{0:T(1024)(128)(4,1)S(1)}, s32[]{:S(2)}) async-start(s8[7077888]{0:T(1024)(128)(4,1)} %bitcast.324), calls=%async_computation.4 | async-start | bytes 5767168
